TPU v7x, 32 devices: a whole 2x2x4 slice. The times are simulated.
32 devices in a mesh: row: 8 (over y, x, core), col: 4 (over z).
Axes of the slice: x: 2, y: 2, z: 4, core: 2. Of those that a mesh axis runs over, the one named last changes fastest.
Arguments:
- ancestor_inverse: float32 [6144, 6144], P('row', 'col'), may hold values from -6 to 6
- factor: float32 [6144, 2560], P('row', 'col'), may hold values from -0.078125 to 0.078125
- diag_inverse: float32 [640, 2560], P('row', 'col'), may hold values from -6 to 6
- widths: int32 [4], replicated, may hold values from 384 to 640
- member: int32 [4, 6144], P(None, 'row'), may hold values 0 or 1
Outputs:
- offdiag: float32 [6144, 2560], P('row', 'col')
- diag_blocks: float32 [640, 2560], P('row', 'col')
All inputs are finite; a program needn't handle non-finite values. No bound on the sum of `member` on one device may be relied on, other than what follows from the above.
Results may differ from a plain program's by a relative error of at most 0.0001.
Values sent between devices are 32-bit elements; how exact they have to be, the bound alone decides.
A program may use at most 128 MiB of HBM per device.

v0:
```python
import jax
import jax.numpy as jnp
from jax import lax
from jax.sharding import PartitionSpec as P

W = 640
NODES = 4


def broadcast(block, axis, holder):
    block = jnp.where(lax.axis_index(axis) == holder, block, jnp.zeros_like(block))
    return lax.psum(block, axis)


def per_device(ancestor_inverse, factor, diag_inverse, widths, member):
    grid_rows = lax.axis_size("row")
    grid_cols = lax.axis_size("col")
    groups = grid_rows // grid_cols
    my_row = lax.axis_index("row")
    my_col = lax.axis_index("col")
    shard_cols = factor.shape[1]
    col_start = my_col * shard_cols
    global_cols = col_start + jnp.arange(shard_cols, dtype=jnp.int32)
    node_of = global_cols // W
    within = global_cols % W
    select = (node_of[:, None] == jnp.arange(NODES, dtype=jnp.int32)[None, :]).astype(jnp.float32)
    width_col = jnp.dot(select, widths.astype(jnp.float32), precision=lax.Precision.HIGHEST)
    col_keep = (within.astype(jnp.float32) < width_col).astype(jnp.float32)
    row_keep = jnp.dot(member.T.astype(jnp.float32), select.T, precision=lax.Precision.HIGHEST)
    mask = row_keep * col_keep[None, :]
    masked = factor * mask
    rows_full = lax.all_gather(masked, "col", axis=1, tiled=True)
    pieces = []
    for offset in range(groups):
        pieces.append(broadcast(rows_full, "row", my_col * groups + offset))
    cols_full = jnp.concatenate(pieces, axis=0)
    partial_product = jnp.dot(
        ancestor_inverse,
        cols_full,
        precision=lax.Precision.HIGHEST,
        preferred_element_type=jnp.float32,
    )
    product = lax.psum_scatter(partial_product, "col", scatter_dimension=1, tiled=True)
    offdiag = -product * mask
    node_start = col_start // W * W
    left = lax.dynamic_slice_in_dim(rows_full, node_start, W, 1)
    local_gram = lax.dot_general(
        left,
        product,
        (((0,), (0,)), ((), ())),
        precision=lax.Precision.HIGHEST,
        preferred_element_type=jnp.float32,
    )
    gram = lax.psum_scatter(local_gram, "row", scatter_dimension=0, tiled=True)
    diag_rows_count = diag_inverse.shape[0]
    local_rows = my_row * diag_rows_count + jnp.arange(diag_rows_count, dtype=jnp.int32)
    inside = (local_rows.astype(jnp.float32)[:, None] < width_col[None, :]).astype(jnp.float32)
    diag_blocks = (diag_inverse + gram) * inside * col_keep[None, :]
    return (offdiag, diag_blocks)


def solution(mesh):
    in_specs = (P("row", "col"), P("row", "col"), P("row", "col"), P(), P(None, "row"))
    out_specs = (P("row", "col"), P("row", "col"))
    return jax.shard_map(
        per_device, mesh=mesh, in_specs=in_specs, out_specs=out_specs, check_vma=False
    )
```

profile of v0, /device:TPU:0, one launch (start us, length us, event | category | flops | bytes accessed | tf_op | source)
XLA Modules:
  0.0 610.8 jit_solution(1386914071417419135)
XLA Ops:
  7.2 0.0 all-gather.2.cloned.1.call-start
  7.2 1.0 convolution_reduce_fusion
  8.3 0.0 copy-start.1
  8.3 2.8 copy.7
  11.1 0.0 copy-done.1
  11.1 3.8 bitcast_multiply_fusion.1
  15.0 0.0 all-gather.2.cloned.1.call-update
  15.0 0.0 all-reduce.3.cloned.1.call-start
  15.1 143.9 %all-gather.2.cloned.1.call-done = f32[768,2560]{0,1:T(8,128)} async-done(((f32[768,640]{0,1:T(8,128)}), f32[768,2560]{0,1:T(8,128)}) %all-gather.2.cloned.1.call-update) | async-done | bytes 7864336 | tf_op jit(solution)/shard_map/all_gather | solution.py:32
  158.9 9.7 %broadcast_select_fusion.1 = (f32[768,2560]{0,1:T(8,128)}, f32[768,2560]{0,1:T(8,128)}) fusion(f32[768,2560]{0,1:T(8,128)} %all-gather.2.cloned.1.call-done, pred[]{:T(512)S(6)} %eq.21, pred[]{:T(512)S(6)} %eq.25), kind=kLoop, calls=%fused_computation.6 | loop fusion | flops 3932160 | bytes 23592962 | tf_op jit(solution)/shard_map/jit(_where)/select_n | solution.py:11
  168.7 0.0 all-reduce.3.cloned.1.call-update
  168.7 0.0 reduce-scatter.3.cloned.1.call-start
  168.7 204.6 %all-reduce.3.cloned.1.call-done = (f32[768,2560]{0,1:T(8,128)}, f32[768,2560]{0,1:T(8,128)}) async-done(((f32[768,2560]{0,1:T(8,128)}, f32[768,2560]{0,1:T(8,128)}), (f32[768,2560]{0,1:T(8,128)}, f32[768,2560]{0,1:T(8,128)})) %all-reduce.3.cloned.1.call-update) | async-done | bytes 15728656 | tf_op jit(solution)/shard_map/psum | solution.py:12
  373.3 45.2 %fusion.4 = f32[768,2560]{0,1:T(8,128)} fusion(f32[768,1536]{1,0:T(8,128)} %param.5, f32[768,2560]{0,1:T(8,128)} %get-tuple-element.4, f32[768,2560]{0,1:T(8,128)} %get-tuple-element.5), kind=kOutput, calls=%fused_computation.4 | convolution fusion | flops 36242718720 | bytes 28311552 | tf_op jit(solution)/shard_map/dot_general | solution.py:37
  418.5 0.0 reduce-scatter.3.cloned.1.call-update
  418.5 0.0 reduce-scatter.5.cloned.1.call-start
  418.6 136.5 %reduce-scatter.3.cloned.1.call-done = f32[768,640]{0,1:T(8,128)} async-done(((f32[768,2560]{0,1:T(8,128)}), f32[768,640]{0,1:T(8,128)}) %reduce-scatter.3.cloned.1.call-update) | async-done | bytes 1966096 | tf_op jit(solution)/shard_map/reduce_scatter | solution.py:43
  555.0 8.2 %fusion.7 = f32[640,640]{1,0:T(8,128)} fusion(f32[768,640]{0,1:T(8,128)} %reduce-scatter.3.cloned.1.call-done, f32[768,2560]{0,1:T(8,128)} %all-gather.2.cloned.1.call-done, s32[]{:T(128)S(6)} %select_n.44), kind=kOutput, calls=%fused_computation.9 | convolution fusion | flops 3774873600 | bytes 5570564 | tf_op jit(solution)/shard_map/dot_general | solution.py:47
  563.2 0.0 reduce-scatter.5.cloned.1.call-update
  563.2 3.1 bitcast_multiply_fusion
  566.4 2.9 copy.8
  569.2 33.3 %reduce-scatter.5.cloned.1.call-done = f32[80,640]{1,0:T(8,128)} async-done(((f32[640,640]{1,0:T(8,128)}), f32[80,640]{1,0:T(8,128)}) %reduce-scatter.5.cloned.1.call-update) | async-done | bytes 204816 | tf_op jit(solution)/shard_map/reduce_scatter | solution.py:54
  602.6 0.0 copy-done
  602.6 1.7 select_multiply_fusion
  (4 shorter events, 0.0 us)
Async XLA Ops:
  7.2 151.8 %all-gather.2.cloned.1.call-start = ((), (), s32[]{:S(2)}) async-start(), calls=%async_computation.2 | async-start | bytes 9830400 | tf_op jit(solution)/shard_map/all_gather | solution.py:32
  8.3 2.8 copy-start.1
  15.0 358.3 %all-reduce.3.cloned.1.call-start = ((), (), s32[]{:S(2)}) async-start(), calls=%async_computation.5 | async-start | bytes 31457280 | tf_op jit(solution)/shard_map/psum | solution.py:12
  168.7 386.4 %reduce-scatter.3.cloned.1.call-start = ((), (), s32[]{:S(2)}) async-start(), calls=%async_computation.3 | async-start | bytes 9830400 | tf_op jit(solution)/shard_map/reduce_scatter | solution.py:43
  418.5 184.1 %reduce-scatter.5.cloned.1.call-start = ((), (), s32[]{:S(2)}) async-start(), calls=%async_computation.4 | async-start | bytes 1843200 | tf_op jit(solution)/shard_map/reduce_scatter | solution.py:54
  566.4 36.2 %copy-start = (f32[80,640]{1,0:T(8,128)S(1)}, f32[80,640]{1,0:T(8,128)}, u32[]{:S(2)}) copy-start(f32[80,640]{1,0:T(8,128)} %param.7) | copy-start | bytes 614404
Sparse Core Ops, SparseCore 0:
  15.1 143.7 all-gather.1
  168.8 204.4 all-reduce.2
  418.6 136.3 reduce-scatter.2
  563.3 39.1 reduce-scatter.4
where the time goes:
time: 611 us
  waiting for transfers between devices  518 us (85%)
  matrix products  58.2 us (10%)
  other arithmetic  14.6 us (2%)
  between operations  13.8 us (2%)
    psum x1, waiting for transfers between devices, broadcast(): return lax.psum(block, axis)  205 us
    all_gather x1, waiting for transfers between devices, per_device(): rows_full = lax.all_gather(masked, 'col', axis=1, tiled=True)  144 us
    reduce_scatter x1, waiting for transfers between devices, per_device(): lax.psum_scatter(partial_product, 'col', scatter_dimension=1, tiled=True)  136 us
    dot_general x1, matrix products, per_device(): jnp.dot(ancestor_inverse, cols_full, precision=lax.Precision.HIGHEST, pre...  45.2 us
    reduce_scatter x1, waiting for transfers between devices, per_device(): gram = lax.psum_scatter(local_gram, 'row', scatter_dimension=0, tiled=True)  33.3 us
  transfers between devices with their start and end apart: 4, of which 4 were waited for; matrix products, arithmetic and copies ran while one was open for 1% of the time, Pallas kernels for 0%

commit v1 on v0

--- a/solution.py
+++ b/solution.py
@@ -5,6 +5,16 @@
 
 W = 640
 NODES = 4
+
+
+def turned_line(shard, axis, along):
+    size = lax.axis_size(axis)
+    held, pieces = (shard, [shard])
+    for _ in range(size - 1):
+        held = lax.ppermute(held, axis, [(i, (i + 1) % size) for i in range(size)])
+        pieces.insert(0, held)
+    line = jnp.concatenate(pieces, axis=along)
+    return jnp.roll(line, (lax.axis_index(axis) + 1) * shard.shape[along], axis=along)
 
 
 def broadcast(block, axis, holder):
@@ -29,7 +39,7 @@
     row_keep = jnp.dot(member.T.astype(jnp.float32), select.T, precision=lax.Precision.HIGHEST)
     mask = row_keep * col_keep[None, :]
     masked = factor * mask
-    rows_full = lax.all_gather(masked, "col", axis=1, tiled=True)
+    rows_full = turned_line(masked, "col", 1)
     pieces = []
     for offset in range(groups):
         pieces.append(broadcast(rows_full, "row", my_col * groups + offset))

time: 611 us -> 625 us (1.023)
  local copies, waits for them, and re-layouts: 5.71 us -> 24.6 us
  waiting for transfers between devices: 518 us -> 510 us
    all_gather x1 -> x0, waiting for transfers between devices: 144 us -> none  [per_device(): rows_full = lax.all_gather(masked, 'col', axis=1, tiled=True)]
    ppermute x0 -> x3, waiting for transfers between devices: none -> 136 us  [turned_line(): held = lax.ppermute(held, axis, [(i, (i + 1) % size) for i in range(size)])]
    unnamed x6 -> x17, local copies, waits for them, and re-layouts: 5.71 us -> 23.2 us
  transfers between devices with their start and end apart: 4 -> 6, of which waited for: 4 -> 6; matrix products, arithmetic and copies ran while one was open for 1% -> 1% of each run, Pallas kernels for 0% -> 0%
where the time goes in v1:
time: 625 us; the launch traced here: 624 us
  waiting for transfers between devices  510 us (82%)
  matrix products  58.3 us (9%)
  local copies, waits for them, and re-layouts  24.6 us (4%)
  other arithmetic  14.6 us (2%)
  between operations  13.8 us (2%)
    psum x1, waiting for transfers between devices, broadcast(): return lax.psum(block, axis)  204 us
    reduce_scatter x1, waiting for transfers between devices, per_device(): lax.psum_scatter(partial_product, 'col', scatter_dimension=1, tiled=True)  136 us
    ppermute x3, waiting for transfers between devices, turned_line(): held = lax.ppermute(held, axis, [(i, (i + 1) % size) for i in range(size)])  136 us
    dot_general x1, matrix products, per_device(): jnp.dot(ancestor_inverse, cols_full, precision=lax.Precision.HIGHEST, pre...  45.2 us
    reduce_scatter x1, waiting for transfers between devices, per_device(): gram = lax.psum_scatter(local_gram, 'row', scatter_dimension=0, tiled=True)  33.3 us
    unnamed x17, local copies, waits for them, and re-layouts  23.2 us
  transfers between devices with their start and end apart: 6, of which 6 were waited for; matrix products, arithmetic and copies ran while one was open for 1% of the time, Pallas kernels for 0%

profile of v1, /device:TPU:0, one launch (start us, length us, event | category | flops | bytes accessed | tf_op | source)
XLA Modules:
  0.0 624.4 jit_solution(3755249591331621308)
XLA Ops:
  8.3 2.8 copy.7
  11.1 3.8 bitcast_multiply_fusion.1
  15.0 3.1 collective-permute-start
  18.0 44.8 %collective-permute-done = f32[768,640]{0,1:T(8,128)S(1)} collective-permute-done((f32[768,640]{0,1:T(8,128)S(1)}, f32[768,640]{0,1:T(8,128)S(1)}, u32[]{:S(2)}, u32[]{:S(2)}) %collective-permute-start) | collective-permute-done | bytes 1966112 | tf_op jit(solution)/shard_map/ppermute | solution.py:14
  62.9 1.3 copy-done.1
  64.2 45.9 %collective-permute-done.1 = f32[768,640]{0,1:T(8,128)} collective-permute-done((f32[768,640]{0,1:T(8,128)S(1)}, f32[768,640]{0,1:T(8,128)}, u32[]{:S(2)}, u32[]{:S(2)}) %collective-permute-start.1) | collective-permute-done | bytes 1966112 | tf_op jit(solution)/shard_map/ppermute | solution.py:14
  110.1 45.2 %collective-permute-done.2 = f32[768,640]{0,1:T(8,128)} collective-permute-done((f32[768,640]{0,1:T(8,128)}, f32[768,640]{0,1:T(8,128)}, u32[]{:S(2)}, u32[]{:S(2)}) %collective-permute-start.2) | collective-permute-done | bytes 1966112 | tf_op jit(solution)/shard_map/ppermute | solution.py:14
  155.3 3.0 constant_dynamic-update-slice_fusion.7
  158.3 2.9 constant_dynamic-update-slice_fusion.6
  161.2 1.4 constant_dynamic-update-slice_fusion.5
  162.6 1.4 constant_dynamic-update-slice_fusion.4
  164.0 3.0 constant_dynamic-update-slice_fusion.3
  167.1 2.9 constant_dynamic-update-slice_fusion.2
  170.0 1.5 constant_dynamic-update-slice_fusion.1
  171.5 1.4 constant_dynamic-update-slice_fusion
  172.9 9.7 %dynamic-slice_select_fusion.1 = (f32[768,2560]{0,1:T(8,128)}, f32[768,2560]{0,1:T(8,128)}) fusion(f32[768,5120]{0,1:T(8,128)} %constant_dynamic-update-slice_fusion, s32[]{:T(128)S(6)} %select_n.57, pred[]{:T(512)S(6)} %eq.24, pred[]{:T(512)S(6)} %eq.28), kind=kLoop, calls=%fused_computation.5 | loop fusion | flops 3932160 | bytes 23592966 | tf_op jit(solution)/shard_map/jit(_where)/select_n | solution.py:21
  182.7 204.2 %all-reduce.3.cloned.1.call-done = (f32[768,2560]{0,1:T(8,128)}, f32[768,2560]{0,1:T(8,128)}) async-done(((f32[768,2560]{0,1:T(8,128)}, f32[768,2560]{0,1:T(8,128)}), (f32[768,2560]{0,1:T(8,128)}, f32[768,2560]{0,1:T(8,128)})) %all-reduce.3.cloned.1.call-update) | async-done | bytes 15728656 | tf_op jit(solution)/shard_map/psum | solution.py:22
  386.9 45.2 %fusion.4 = f32[768,2560]{0,1:T(8,128)} fusion(f32[768,1536]{1,0:T(8,128)} %param.5, f32[768,2560]{0,1:T(8,128)} %get-tuple-element.4, f32[768,2560]{0,1:T(8,128)} %get-tuple-element.5), kind=kOutput, calls=%fused_computation.6 | convolution fusion | flops 36242718720 | bytes 28311552 | tf_op jit(solution)/shard_map/dot_general | solution.py:47
  432.3 136.3 %reduce-scatter.3.cloned.1.call-done = f32[768,640]{0,1:T(8,128)} async-done(((f32[768,2560]{0,1:T(8,128)}), f32[768,640]{0,1:T(8,128)}) %reduce-scatter.3.cloned.1.call-update) | async-done | bytes 1966096 | tf_op jit(solution)/shard_map/reduce_scatter | solution.py:53
  568.6 8.2 %fusion.7 = f32[640,640]{1,0:T(8,128)} fusion(f32[768,640]{0,1:T(8,128)} %reduce-scatter.3.cloned.1.call-done, f32[768,5120]{0,1:T(8,128)} %constant_dynamic-update-slice_fusion, s32[]{:T(128)S(6)} %dynamic_slice.11), kind=kOutput, calls=%fused_computation.9 | convolution fusion | flops 3774873600 | bytes 5570564 | tf_op jit(solution)/shard_map/dot_general | solution.py:57
  576.9 3.1 bitcast_multiply_fusion
  580.0 2.8 copy.8
  582.8 33.3 %reduce-scatter.5.cloned.1.call-done = f32[80,640]{1,0:T(8,128)} async-done(((f32[640,640]{1,0:T(8,128)}), f32[80,640]{1,0:T(8,128)}) %reduce-scatter.5.cloned.1.call-update) | async-done | bytes 204816 | tf_op jit(solution)/shard_map/reduce_scatter | solution.py:64
  616.2 1.7 select_multiply_fusion
  (19 shorter events, 1.4 us)
Async XLA Ops:
  7.2 379.7 %all-reduce.3.cloned.1.call-start = ((), (), s32[]{:S(2)}) async-start(), calls=%async_computation.4 | async-start | bytes 31457280 | tf_op jit(solution)/shard_map/psum | solution.py:22
  15.0 47.9 %collective-permute-start = (f32[768,640]{0,1:T(8,128)S(1)}, f32[768,640]{0,1:T(8,128)S(1)}, u32[]{:S(2)}, u32[]{:S(2)}) collective-permute-start(f32[768,640]{0,1:T(8,128)S(1)} %get-tuple-element.8), channel_id=1, source_target_pairs={{0,1},{1,2},{2,3},{3,0},{4,5},{5,6},{6,7},{7,4},{8,9},{9,10},{10,1... | collective-permute-start | bytes 5898248 | tf_op jit(solution)/shard_map/ppermute | solution.py:14
  62.9 1.3 copy-start.1
  64.2 45.9 %collective-permute-start.1 = (f32[768,640]{0,1:T(8,128)S(1)}, f32[768,640]{0,1:T(8,128)}, u32[]{:S(2)}, u32[]{:S(2)}) collective-permute-start(f32[768,640]{0,1:T(8,128)S(1)} %collective-permute-done), channel_id=1, source_target_pairs={{0,1},{1,2},{2,3},{3,0},{4,5},{5,6},{6,7},{7,4},{8,9},{9,10},{10,1... | collective-permute-start | bytes 5898248 | tf_op jit(solution)/shard_map/ppermute | solution.py:14
  110.0 45.2 %collective-permute-start.2 = (f32[768,640]{0,1:T(8,128)}, f32[768,640]{0,1:T(8,128)}, u32[]{:S(2)}, u32[]{:S(2)}) collective-permute-start(f32[768,640]{0,1:T(8,128)} %collective-permute-done.1), channel_id=1, source_target_pairs={{0,1},{1,2},{2,3},{3,0},{4,5},{5,6},{6,7},{7,4},{8,9},{9,10},{10,1... | collective-permute-start | bytes 5898248 | tf_op jit(solution)/shard_map/ppermute | solution.py:14
  110.0 51.2 %copy-start.2 = (f32[768,640]{0,1:T(8,128)S(1)}, f32[768,640]{0,1:T(8,128)}, u32[]{:S(2)}) copy-start(f32[768,640]{0,1:T(8,128)} %copy-done.1) | copy-start | bytes 5898244
  182.7 386.0 %reduce-scatter.3.cloned.1.call-start = ((), (), s32[]{:S(2)}) async-start(), calls=%async_computation.2 | async-start | bytes 9830400 | tf_op jit(solution)/shard_map/reduce_scatter | solution.py:53
  432.0 144.9 %copy-start = (f32[640,768]{1,0:T(8,128)S(1)}, f32[640,768]{1,0:T(8,128)}, u32[]{:S(2)}) copy-start(f32[640,768]{1,0:T(8,128)} %get-tuple-element.9) | copy-start | bytes 5898244
  432.1 184.1 %reduce-scatter.5.cloned.1.call-start = ((), (), s32[]{:S(2)}) async-start(), calls=%async_computation.3 | async-start | bytes 1843200 | tf_op jit(solution)/shard_map/reduce_scatter | solution.py:64
  432.3 183.8 %copy-start.3 = (f32[80,640]{1,0:T(8,128)S(1)}, f32[80,640]{1,0:T(8,128)}, u32[]{:S(2)}) copy-start(f32[80,640]{1,0:T(8,128)} %param.7) | copy-start | bytes 614404
Sparse Core Ops, SparseCore 0:
  182.8 204.0 all-reduce.2
  432.2 136.4 reduce-scatter.2
  577.0 39.1 reduce-scatter.4
